TPU v7x, 32 devices: a whole 2x2x4 slice. The times are simulated.
32 devices in a mesh: row: 16 (over z, y, core), col: 2 (over x).
Axes of the slice: x: 2, y: 2, z: 4, core: 2. Of those that a mesh axis runs over, the one named last changes fastest.
Arguments:
- node_features: float32 [4096, 128], P(('row', 'col')), may hold values from -6 to 6
- block_values: float32 [16, 2, 4, 128, 128], P('row', 'col')
- block_rows: int32 [16, 2, 4], P('row', 'col'), may hold values from 0 to 1, as said below
- block_cols: int32 [16, 2, 4], P('row', 'col'), may hold values from 0 to 15
- block_count: int32 [16, 2], P('row', 'col'), may hold values from 1 to 4, as said below
- w_input: float32 [128, 512], replicated, may hold values from -0.5 to 0.5
- bias_input: float32 [512], replicated, may hold values from -3 to 3
- gain_attn: float32 [512], replicated, may hold values from 0.1 to 1.9
- shift_attn: float32 [512], replicated, may hold values from -3 to 3
- w_heads: float32 [512, 1536], replicated, may hold values from -0.25 to 0.25
- w_merge: float32 [512, 512], replicated, may hold values from -0.75 to 0.75
- bias_merge: float32 [512], replicated, may hold values from -3 to 3
- gain_ffn: float32 [512], replicated, may hold values from 0.1 to 1.9
- shift_ffn: float32 [512], replicated, may hold values from -3 to 3
- w_expand: float32 [512, 1024], replicated, may hold values from -0.25 to 0.25
- bias_expand: float32 [1024], replicated, may hold values from -3 to 3
- w_reduce: float32 [1024, 512], replicated, may hold values from -0.25 to 0.25
- bias_reduce: float32 [512], replicated, may hold values from -3 to 3
- readout: float32 [512], replicated, may hold values from -0.25 to 0.25
- cotangent: float32 [4096, 512], P(('row', 'col')), may hold values from -6 to 6
Outputs:
- layer_out: float32 [4096, 512], P(('row', 'col'))
- grad_features: float32 [4096, 128], P(('row', 'col'))
- grad_w_input: float32 [128, 512], replicated
- grad_bias_input: float32 [512], replicated
- grad_gain_attn: float32 [512], replicated
- grad_shift_attn: float32 [512], replicated
- grad_w_heads: float32 [512, 1536], replicated
- grad_w_merge: float32 [512, 512], replicated
- grad_bias_merge: float32 [512], replicated
- grad_gain_ffn: float32 [512], replicated
- grad_shift_ffn: float32 [512], replicated
- grad_w_expand: float32 [512, 1024], replicated
- grad_bias_expand: float32 [1024], replicated
- grad_w_reduce: float32 [1024, 512], replicated
- grad_bias_reduce: float32 [512], replicated
- grad_readout: float32 [512], replicated
Inputs may be any that keep to these rules, and one draw needn't show every extreme that they name: Within one tile the listed (block_rows, block_cols) pairs are all different. Slots 0 to block_count - 1 of a tile are live, the rest are ignored; some tile has all 4 slots live.
All inputs are finite; a program needn't handle non-finite values.
Results may differ from a plain program's by a relative error of at most 0.0003.
Values sent between devices are 32-bit elements; how exact they have to be, the bound alone decides.
No kernel may reach another device: no remote copies, remote signals or barrier semaphores. Data moves between devices by JAX's collectives and lax.ppermute only.
A program may use at most 192 MiB of HBM per device.

v0:
```python
import math
import jax
import jax.numpy as jnp
from jax import lax
from jax.sharding import PartitionSpec as P

HEADS = 8
HEAD_DIM = 64
HOPS = 7
exact = lax.Precision.HIGHEST


def layer_norm(values, gain, shift):
    average = jnp.mean(values, axis=-1, keepdims=True)
    centred = values - average
    spread = jnp.mean(centred * centred, axis=-1, keepdims=True)
    return centred * lax.rsqrt(spread + 1e-05) * gain + shift


def node_tail(
    start,
    gain_attn,
    shift_attn,
    w_heads,
    w_merge,
    bias_merge,
    gain_ffn,
    shift_ffn,
    w_expand,
    bias_expand,
    w_reduce,
    bias_reduce,
    readout,
):
    node_count, token_count, columns = start.shape
    normed = layer_norm(start, gain_attn, shift_attn)
    projected = jnp.einsum("ntd,de->nte", normed, w_heads, precision=exact)
    queries = projected[..., :columns].reshape(node_count, token_count, HEADS, HEAD_DIM)
    key_rows = projected[..., columns : 2 * columns].reshape(
        node_count, token_count, HEADS, HEAD_DIM
    )
    value_rows = projected[..., 2 * columns :].reshape(node_count, token_count, HEADS, HEAD_DIM)
    scores = jnp.einsum("nqhe,nkhe->nhqk", queries, key_rows, precision=exact) / math.sqrt(HEAD_DIM)
    attention = jax.nn.softmax(scores, axis=-1)
    mixed = jnp.einsum("nhqk,nkhe->nqhe", attention, value_rows, precision=exact).reshape(
        node_count, token_count, columns
    )
    middle = start + jnp.einsum("ntd,de->nte", mixed, w_merge, precision=exact) + bias_merge
    normed_two = layer_norm(middle, gain_ffn, shift_ffn)
    activated = jax.nn.gelu(
        jnp.einsum("ntd,de->nte", normed_two, w_expand, precision=exact) + bias_expand,
        approximate=False,
    )
    final = middle + jnp.einsum("nte,ed->ntd", activated, w_reduce, precision=exact) + bias_reduce
    center = final[:, 0]
    others = final[:, 1:]
    weights = jax.nn.softmax(jnp.einsum("nkd,d->nk", others, readout, precision=exact), axis=-1)
    return center + jnp.einsum("nk,nkd->nd", weights, others, precision=exact)


def per_device(
    node_features,
    block_values,
    block_rows,
    block_cols,
    block_count,
    w_input,
    bias_input,
    gain_attn,
    shift_attn,
    w_heads,
    w_merge,
    bias_merge,
    gain_ffn,
    shift_ffn,
    w_expand,
    bias_expand,
    w_reduce,
    bias_reduce,
    readout,
    cotangent,
):
    values = block_values[0, 0]
    row_ids = block_rows[0, 0]
    col_ids = block_cols[0, 0]
    block_size = values.shape[-1]
    node_count = node_features.shape[0]
    row_blocks = lax.axis_size("col") * node_count // block_size
    col_blocks = lax.axis_size("row") * node_count // block_size
    is_live = (jnp.arange(values.shape[0]) < block_count[0, 0]).astype(jnp.float32)
    row_table = (row_ids[:, None] == jnp.arange(row_blocks)[None, :]).astype(jnp.float32) * is_live[
        :, None
    ]
    col_table = (col_ids[:, None] == jnp.arange(col_blocks)[None, :]).astype(jnp.float32) * is_live[
        :, None
    ]
    hop_list = [node_features]
    for hop_index in range(HOPS):
        field = hop_list[-1]
        forward_columns = field.shape[1]
        forward_gathered = lax.all_gather(field, "row", axis=0, tiled=True).reshape(
            col_blocks, block_size, forward_columns
        )
        forward_picked = forward_gathered[col_ids]
        forward_products = jnp.einsum("bij,bjw->biw", values, forward_picked, precision=exact)
        forward_partial_value = jnp.einsum(
            "br,biw->riw", row_table, forward_products, precision=exact
        ).reshape(row_blocks * block_size, forward_columns)
        hop_list.append(
            lax.psum_scatter(forward_partial_value, "col", scatter_dimension=0, tiled=True)
        )
    stacked = jnp.stack(hop_list, axis=1)

    def local_layer(
        stacked_hops,
        w_input,
        bias_input,
        gain_attn,
        shift_attn,
        w_heads,
        w_merge,
        bias_merge,
        gain_ffn,
        shift_ffn,
        w_expand,
        bias_expand,
        w_reduce,
        bias_reduce,
        readout,
    ):
        start = jnp.einsum("ntf,fd->ntd", stacked_hops, w_input, precision=exact) + bias_input
        return node_tail(
            start,
            gain_attn,
            shift_attn,
            w_heads,
            w_merge,
            bias_merge,
            gain_ffn,
            shift_ffn,
            w_expand,
            bias_expand,
            w_reduce,
            bias_reduce,
            readout,
        )

    layer_out, pullback = jax.vjp(
        local_layer,
        stacked,
        w_input,
        bias_input,
        gain_attn,
        shift_attn,
        w_heads,
        w_merge,
        bias_merge,
        gain_ffn,
        shift_ffn,
        w_expand,
        bias_expand,
        w_reduce,
        bias_reduce,
        readout,
    )
    (
        grad_hops,
        grad_w_input,
        grad_bias_input,
        grad_gain_attn,
        grad_shift_attn,
        grad_w_heads,
        grad_w_merge,
        grad_bias_merge,
        grad_gain_ffn,
        grad_shift_ffn,
        grad_w_expand,
        grad_bias_expand,
        grad_w_reduce,
        grad_bias_reduce,
        grad_readout,
    ) = pullback(cotangent)
    carried = grad_hops[:, HOPS]
    for hop_index in range(HOPS - 1, -1, -1):
        columns = carried.shape[1]
        gathered = lax.all_gather(carried, "col", axis=0, tiled=True).reshape(
            row_blocks, block_size, columns
        )
        picked = gathered[row_ids]
        products = jnp.einsum("bji,bjw->biw", values, picked, precision=exact)
        partial_value = jnp.einsum("bc,biw->ciw", col_table, products, precision=exact).reshape(
            col_blocks * block_size, columns
        )
        carried = grad_hops[:, hop_index] + lax.psum_scatter(
            partial_value, "row", scatter_dimension=0, tiled=True
        )
    summed = lax.psum(
        (
            grad_w_input,
            grad_bias_input,
            grad_gain_attn,
            grad_shift_attn,
            grad_w_heads,
            grad_w_merge,
            grad_bias_merge,
            grad_gain_ffn,
            grad_shift_ffn,
            grad_w_expand,
            grad_bias_expand,
            grad_w_reduce,
            grad_bias_reduce,
            grad_readout,
        ),
        ("row", "col"),
    )
    return (
        layer_out,
        carried,
        summed[0],
        summed[1],
        summed[2],
        summed[3],
        summed[4],
        summed[5],
        summed[6],
        summed[7],
        summed[8],
        summed[9],
        summed[10],
        summed[11],
        summed[12],
        summed[13],
    )


def solution(mesh):
    placed = (
        P(("row", "col"), None),
        P("row", "col", None, None, None),
        P("row", "col", None),
        P("row", "col", None),
        P("row", "col"),
        P(),
        P(),
        P(),
        P(),
        P(),
        P(),
        P(),
        P(),
        P(),
        P(),
        P(),
        P(),
        P(),
        P(),
        P(("row", "col"), None),
    )
    return jax.shard_map(
        per_device,
        mesh=mesh,
        in_specs=placed,
        out_specs=(
            P(("row", "col"), None),
            P(("row", "col"), None),
            P(),
            P(),
            P(),
            P(),
            P(),
            P(),
            P(),
            P(),
            P(),
            P(),
            P(),
            P(),
            P(),
            P(),
        ),
        check_vma=False,
    )
```

profile of v0, /device:TPU:0, one launch (start us, length us, event | category | flops | bytes accessed | tf_op | source)
XLA Modules:
  0.0 1398.2 jit_solution(17185425207712821760)
XLA Ops:
  9.5 41.4 %all-gather.9.cloned.1.call-done = f32[2048,128]{1,0:T(8,128)} async-done(((f32[128,128]{1,0:T(8,128)}), f32[2048,128]{1,0:T(8,128)}) %all-gather.9.cloned.1.call-update) | async-done | bytes 1048592 | tf_op jit(solution)/shard_map/all_gather | solution.py:101
  59.8 9.3 reduce-scatter.15.cloned.1.call-done
  69.1 40.1 %all-gather.11.cloned.1.call-done = f32[2048,128]{1,0:T(8,128)} async-done(((f32[128,128]{1,0:T(8,128)}), f32[2048,128]{1,0:T(8,128)}) %all-gather.11.cloned.1.call-update) | async-done | bytes 1048592 | tf_op jit(solution)/shard_map/all_gather | solution.py:101
  127.4 39.9 %all-gather.13.cloned.1.call-done = f32[2048,128]{1,0:T(8,128)} async-done(((f32[128,128]{1,0:T(8,128)}), f32[2048,128]{1,0:T(8,128)}) %all-gather.13.cloned.1.call-update) | async-done | bytes 1048592 | tf_op jit(solution)/shard_map/all_gather | solution.py:101
  176.1 9.3 reduce-scatter.19.cloned.1.call-done
  185.4 40.1 %all-gather.15.cloned.1.call-done = f32[2048,128]{1,0:T(8,128)} async-done(((f32[128,128]{1,0:T(8,128)}), f32[2048,128]{1,0:T(8,128)}) %all-gather.15.cloned.1.call-update) | async-done | bytes 1048592 | tf_op jit(solution)/shard_map/all_gather | solution.py:101
  234.3 9.3 reduce-scatter.21.cloned.1.call-done
  243.7 40.1 %all-gather.17.cloned.1.call-done = f32[2048,128]{1,0:T(8,128)} async-done(((f32[128,128]{1,0:T(8,128)}), f32[2048,128]{1,0:T(8,128)}) %all-gather.17.cloned.1.call-update) | async-done | bytes 1048592 | tf_op jit(solution)/shard_map/all_gather | solution.py:101
  301.9 40.1 %all-gather.19.cloned.1.call-done = f32[2048,128]{1,0:T(8,128)} async-done(((f32[128,128]{1,0:T(8,128)}), f32[2048,128]{1,0:T(8,128)}) %all-gather.19.cloned.1.call-update) | async-done | bytes 1048592 | tf_op jit(solution)/shard_map/all_gather | solution.py:101
  366.4 33.8 %all-gather.21.cloned.1.call-done = f32[2048,128]{1,0:T(8,128)} async-done(((f32[128,128]{1,0:T(8,128)}), f32[2048,128]{1,0:T(8,128)}) %all-gather.21.cloned.1.call-update) | async-done | bytes 1048592 | tf_op jit(solution)/shard_map/all_gather | solution.py:101
  424.0 10.8 fusion.10
  434.9 14.4 %fusion.197 = (f32[128,8,512]{2,0,1:T(8,128)}, f32[128,8,512]{2,0,1:T(8,128)}, f32[128,8,512]{2,0,1:T(8,128)}) fusion(f32[128,8,1536]{2,0,1:T(8,128)S(1)} %fusion.10), kind=kLoop, calls=%fused_computation.285 | loop fusion | bytes 12582912 | tf_op jit(solution)/shard_map/jvp()/slice | solution.py:39
  474.8 9.8 multiply_reduce_fusion.1
  488.8 10.2 convolution_bitcast_fusion.3
  519.2 9.3 fusion.2
  549.4 14.6 %fusion.199 = (f32[1024]{0:T(1024)}, f32[128,8,1024]{2,0,1:T(8,128)S(1)}) fusion(f32[128,8,1024]{2,0,1:T(8,128)} %copy-done.9, f32[1024,512]{1,0:T(8,128)} %param.36, f32[128,1,512]{2,0,1:T(8,128)} %bitcast.328, f32[128,7,512]{2,0,1:T(8,128)S(1)} %multiply_add_fusion.3, f32[128,8,1024]{2,0,1:T(8,128)} %copy-done.7, f32[1024]{0:T(1024)S(1)} %copy-done.43), kind=kOutput, calls=%fused_computation.287 | convolution fusion | flops 6458702848 | bytes 16785408 | tf_op jit(solution)/shard_map/transpose(jvp(nte,ed->ntd))/dot_general | solution.py:54
  587.0 16.1 %multiply_reduce_fusion = (f32[128,8,8]{2,1,0:T(8,128)}, f32[128,8,8,8]{2,3,1,0:T(8,128)}) fusion(f32[128,8,8]{2,1,0:T(8,128)} %multiply_divide_fusion, f32[128,8,8]{2,1,0:T(8,128)} %copy-done.20, f32[128,8,8,8]{2,3,1,0:T(8,128)} %copy-done.10, f32[128,8,64,8]{2,3,1,0:T(8,128)} %copy.74, f32[128,8,8,64]{3,1,2,0:T(8,128)} %copy.69), kind=kOutput, calls=%fused_computation.25 | convolution fusion | flops 50651136 | bytes 4816896 | tf_op jit(solution)/shard_map/transpose(jvp(nhqk,nkhe->nqhe))/dot_general | solution.py:45
  605.0 12.5 convolution_bitcast_fusion
  617.5 14.7 %convolution_bitcast_fusion.1 = f32[128,8,8,64]{3,1,2,0:T(8,128)} fusion(f32[128,8,8,64]{3,1,2,0:T(8,128)} %copy.67, f32[128,8,8,8]{2,3,1,0:T(8,128)} %get-tuple-element.59, f32[128,8,8]{2,1,0:T(8,128)} %copy-done.39, f32[128,8,8]{2,1,0:T(8,128)S(1)} %copy-done.30, f32[128,8,8]{2,1,0:T(8,128)S(1)} %copy-done.21, f32[128,8,8,8]{2,3,1,0:T(8,128)} %copy-done.10), kind=kOutput, calls=%fused_computation.49 | convolution fusion | flops 50724864 | bytes 4816896 | tf_op jit(solution)/shard_map/transpose(jvp(nqhe,nkhe->nhqk))/dot_general | solution.py:43
  632.2 13.5 convolution_bitcast_fusion.2
  659.9 24.2 %fusion.194 = (f32[512]{0:T(512)}, f32[128,8]{0,1:T(8,128)S(1)}, f32[128,8,512]{2,0,1:T(8,128)S(1)}) fusion(f32[512]{0:T(512)S(1)} %copy-done.55, f32[128,8]{0,1:T(8,128)S(1)} %broadcast_multiply_fusion.1, f32[128,8,512]{2,0,1:T(8,128)} %copy-done.3, f32[512]{0:T(512)S(1)} %copy-done.42, f32[512,1536]{1,0:T(8,128)S(1)} %copy-done, ...), kind=kOutput, calls=%fused_computation.282 | convolution fusion | flops 9669965824 | bytes 13645824 | tf_op jit(solution)/shard_map/transpose(jvp(ntd,de->nte))/dot_general | solution.py:37
  705.3 57.6 %reduce-scatter.29.cloned.1.call-done = f32[128,128]{1,0:T(8,128)} async-done(((f32[2048,128]{1,0:T(8,128)}), f32[128,128]{1,0:T(8,128)}) %reduce-scatter.29.cloned.1.call-update) | async-done | bytes 65552 | tf_op jit(solution)/shard_map/reduce_scatter | solution.py:194
  777.6 56.5 %reduce-scatter.31.cloned.1.call-done = f32[128,128]{1,0:T(8,128)} async-done(((f32[2048,128]{1,0:T(8,128)}), f32[128,128]{1,0:T(8,128)}) %reduce-scatter.31.cloned.1.call-update) | async-done | bytes 65552 | tf_op jit(solution)/shard_map/reduce_scatter | solution.py:194
  848.9 56.5 %reduce-scatter.33.cloned.1.call-done = f32[128,128]{1,0:T(8,128)} async-done(((f32[2048,128]{1,0:T(8,128)}), f32[128,128]{1,0:T(8,128)}) %reduce-scatter.33.cloned.1.call-update) | async-done | bytes 65552 | tf_op jit(solution)/shard_map/reduce_scatter | solution.py:194
  920.1 56.5 %reduce-scatter.35.cloned.1.call-done = f32[128,128]{1,0:T(8,128)} async-done(((f32[2048,128]{1,0:T(8,128)}), f32[128,128]{1,0:T(8,128)}) %reduce-scatter.35.cloned.1.call-update) | async-done | bytes 65552 | tf_op jit(solution)/shard_map/reduce_scatter | solution.py:194
  991.8 56.4 %reduce-scatter.37.cloned.1.call-done = f32[128,128]{1,0:T(8,128)} async-done(((f32[2048,128]{1,0:T(8,128)}), f32[128,128]{1,0:T(8,128)}) %reduce-scatter.37.cloned.1.call-update) | async-done | bytes 65552 | tf_op jit(solution)/shard_map/reduce_scatter | solution.py:194
  1062.9 11.2 fusion.24
  1074.1 45.4 %reduce-scatter.39.cloned.1.call-done = f32[128,128]{1,0:T(8,128)} async-done(((f32[2048,128]{1,0:T(8,128)}), f32[128,128]{1,0:T(8,128)}) %reduce-scatter.39.cloned.1.call-update) | async-done | bytes 65552 | tf_op jit(solution)/shard_map/reduce_scatter | solution.py:194
  1144.3 10.2 convolution_bitcast_fusion.4
  1154.7 22.1 %fusion.8 = f32[512,1536]{1,0:T(8,128)} fusion(f32[128,8,512]{0,2,1:T(8,128)S(1)} %bitcast.343, f32[128,8,512]{0,2,1:T(8,128)S(1)} %bitcast.341, f32[128,8,512]{0,2,1:T(8,128)S(1)} %bitcast.339, f32[512]{0:T(512)S(1)} %copy-done.69, f32[512]{0:T(512)S(1)} %copy-done.56, f32[128,8]{0,1:T(8,128)S(1)} %copy-done.46, f32[128,8,512]{2,0,1:T(8,128)S(1)} %copy-done.5, ...), kind=kOutput, calls=%fused_computation.42 | convolution fusion | flops 9669443584 | bytes 11548672 | tf_op jit(solution)/shard_map/transpose(jvp(ntd,de->nte))/dot_general | solution.py:37
  1180.1 41.8 %all-reduce.5 = (f32[512]{0:T(512)}, f32[512]{0:T(512)}, f32[512]{0:T(512)}, f32[512]{0:T(512)}, f32[512]{0:T(512)}, /*index=5*/f32[512]{0:T(512)}, f32[1024]{0:T(1024)}, f32[512]{0:T(512)}, f32[512]{0:T(512)}) all-reduce(f32[512]{0:T(512)S(1)} %copy-done.60, f32[512]{0:T(512)S(1)} %copy-done.59, ...), channel_id=1, replica_groups=mesh['row'=16,'col'=2] {'row','col'}, use_global_device_ids=true, to_apply=%region_30.0 | all-reduce | flops 5120 | bytes 40960 | tf_op jit(solution)/shard_map/psum | solution.py:197
  1229.5 152.0 %all-reduce.9.cloned.1.call-done = (f32[128,512]{1,0:T(8,128)}, f32[512,1536]{1,0:T(8,128)}, f32[512,512]{1,0:T(8,128)}, f32[512,1024]{1,0:T(8,128)}, f32[1024,512]{1,0:T(8,128)}) async-done(((f32[128,512]{1,0:T(8,128)}, f32[512,1536]{1,0:T(8,128)}, f32[512,512]{1,0:T(8,128)}, f32[512,1024]{1,0:T(8,128)}, f32[1024,512]{1,0:T(8,128)}), (f32[128,512]{1,0:T(8,128)}, f32[512,1536]{1,0:T(8,128)}, ...) | async-done | bytes 8650768 | tf_op jit(solution)/shard_map/psum | solution.py:197
  (345 shorter events, 361.8 us)
Async XLA Ops:
  7.2 416.8 %copy-start = (f32[512,1536]{1,0:T(8,128)S(1)}, f32[512,1536]{1,0:T(8,128)}, u32[]{:S(2)}) copy-start(f32[512,1536]{1,0:T(8,128)} %param.29) | copy-start | bytes 9437188
  7.2 162.6 %copy-start.6 = (f32[1,1,4,128,128]{4,3,2,1,0:T(8,128)S(1)}, f32[1,1,4,128,128]{4,3,2,1,0:T(8,128)}, u32[]{:S(2)}) copy-start(f32[1,1,4,128,128]{4,3,2,1,0:T(8,128)} %param.21) | copy-start | bytes 786436
  7.2 108.6 %copy-start.52 = (s32[1,1,4]{2,1,0:T(1,128)S(1)}, s32[1,1,4]{2,1,0:T(1,128)}, u32[]{:S(2)}) copy-start(s32[1,1,4]{2,1,0:T(1,128)} %param.22) | copy-start | bytes 52
  7.2 43.7 %all-gather.9.cloned.1.call-start = ((), (), s32[]{:S(2)}) async-start(), calls=%async_computation.14 | async-start | bytes 1114112 | tf_op jit(solution)/shard_map/all_gather | solution.py:101
  8.0 61.1 %reduce-scatter.15.cloned.1.call-start = ((), (), s32[]{:S(2)}) async-start(), calls=%async_computation.15 | async-start | bytes 196608 | tf_op jit(solution)/shard_map/reduce_scatter | solution.py:110
  59.7 49.5 %all-gather.11.cloned.1.call-start = ((), (), s32[]{:S(2)}) async-start(), calls=%async_computation.16 | async-start | bytes 1114112 | tf_op jit(solution)/shard_map/all_gather | solution.py:101
  69.1 58.3 %reduce-scatter.17.cloned.1.call-start = ((), (), s32[]{:S(2)}) async-start(), calls=%async_computation.17 | async-start | bytes 196608 | tf_op jit(solution)/shard_map/reduce_scatter | solution.py:110
  118.0 49.3 %all-gather.13.cloned.1.call-start = ((), (), s32[]{:S(2)}) async-start(), calls=%async_computation.18 | async-start | bytes 1114112 | tf_op jit(solution)/shard_map/all_gather | solution.py:101
  127.3 58.0 %reduce-scatter.19.cloned.1.call-start = ((), (), s32[]{:S(2)}) async-start(), calls=%async_computation.19 | async-start | bytes 196608 | tf_op jit(solution)/shard_map/reduce_scatter | solution.py:110
  176.0 184.7 %copy-start.40 = (f32[128,128]{1,0:T(8,128)S(1)}, f32[128,128]{1,0:T(8,128)}, u32[]{:S(2)}) copy-start(f32[128,128]{1,0:T(8,128)} %param.20) | copy-start | bytes 196612
  176.0 185.3 %copy-start.41 = (f32[128,128]{1,0:T(8,128)S(1)}, f32[128,128]{1,0:T(8,128)}, u32[]{:S(2)}) copy-start(f32[128,128]{1,0:T(8,128)} %reduce-scatter.15.cloned.1.call-done) | copy-start | bytes 196612
  176.1 49.5 %all-gather.15.cloned.1.call-start = ((), (), s32[]{:S(2)}) async-start(), calls=%async_computation.20 | async-start | bytes 1114112 | tf_op jit(solution)/shard_map/all_gather | solution.py:101
  185.4 58.2 %reduce-scatter.21.cloned.1.call-start = ((), (), s32[]{:S(2)}) async-start(), calls=%async_computation.21 | async-start | bytes 196608 | tf_op jit(solution)/shard_map/reduce_scatter | solution.py:110
  234.3 49.5 %all-gather.17.cloned.1.call-start = ((), (), s32[]{:S(2)}) async-start(), calls=%async_computation.22 | async-start | bytes 1114112 | tf_op jit(solution)/shard_map/all_gather | solution.py:101
  243.6 58.2 %reduce-scatter.23.cloned.1.call-start = ((), (), s32[]{:S(2)}) async-start(), calls=%async_computation.23 | async-start | bytes 196608 | tf_op jit(solution)/shard_map/reduce_scatter | solution.py:110
  286.2 133.5 %copy-start.42 = (f32[512]{0:T(512)S(1)}, f32[512]{0:T(512)}, u32[]{:S(2)}) copy-start(f32[512]{0:T(512)} %param.26) | copy-start | bytes 6148
  292.5 49.5 %all-gather.19.cloned.1.call-start = ((), (), s32[]{:S(2)}) async-start(), calls=%async_computation.24 | async-start | bytes 1114112 | tf_op jit(solution)/shard_map/all_gather | solution.py:101
  301.8 58.2 %reduce-scatter.25.cloned.1.call-start = ((), (), s32[]{:S(2)}) async-start(), calls=%async_computation.25 | async-start | bytes 196608 | tf_op jit(solution)/shard_map/reduce_scatter | solution.py:110
  350.7 49.5 %all-gather.21.cloned.1.call-start = ((), (), s32[]{:S(2)}) async-start(), calls=%async_computation.26 | async-start | bytes 1114112 | tf_op jit(solution)/shard_map/all_gather | solution.py:101
  360.0 58.2 %reduce-scatter.27.cloned.1.call-start = ((), (), s32[]{:S(2)}) async-start(), calls=%async_computation.27 | async-start | bytes 196608 | tf_op jit(solution)/shard_map/reduce_scatter | solution.py:110
  361.9 62.1 %copy-start.55 = (f32[512]{0:T(512)S(1)}, f32[512]{0:T(512)}, u32[]{:S(2)}) copy-start(f32[512]{0:T(512)} %param.27) | copy-start | bytes 6148
  361.9 62.1 %copy-start.68 = (f32[512]{0:T(512)S(1)}, f32[512]{0:T(512)}, u32[]{:S(2)}) copy-start(f32[512]{0:T(512)} %param.28) | copy-start | bytes 6148
  408.9 354.0 %reduce-scatter.29.cloned.1.call-start = ((), (), s32[]{:S(2)}) async-start(), calls=%async_computation.28 | async-start | bytes 1114112 | tf_op jit(solution)/shard_map/reduce_scatter | solution.py:194
  424.0 262.0 %copy-start.45 = (f32[128,8]{0,1:T(8,128)}, f32[128,8]{0,1:T(8,128)S(1)}, u32[]{:S(2)}) copy-start(f32[128,8]{0,1:T(8,128)S(1)} %fusion.126) | copy-start | bytes 12292
  511.1 62.3 %copy-start.47 = (f32[128,8]{0,1:T(8,128)}, f32[128,8]{0,1:T(8,128)S(1)}, u32[]{:S(2)}) copy-start(f32[128,8]{0,1:T(8,128)S(1)} %fusion.127) | copy-start | bytes 12292
  705.3 128.9 %reduce-scatter.31.cloned.1.call-start = ((), (), s32[]{:S(2)}) async-start(), calls=%async_computation.29 | async-start | bytes 1114112 | tf_op jit(solution)/shard_map/reduce_scatter | solution.py:194
  777.6 127.8 %reduce-scatter.33.cloned.1.call-start = ((), (), s32[]{:S(2)}) async-start(), calls=%async_computation.30 | async-start | bytes 1114112 | tf_op jit(solution)/shard_map/reduce_scatter | solution.py:194
  848.8 127.8 %reduce-scatter.35.cloned.1.call-start = ((), (), s32[]{:S(2)}) async-start(), calls=%async_computation.31 | async-start | bytes 1114112 | tf_op jit(solution)/shard_map/reduce_scatter | solution.py:194
  920.1 128.1 %reduce-scatter.37.cloned.1.call-start = ((), (), s32[]{:S(2)}) async-start(), calls=%async_computation.32 | async-start | bytes 1114112 | tf_op jit(solution)/shard_map/reduce_scatter | solution.py:194
  991.7 127.8 %reduce-scatter.39.cloned.1.call-start = ((), (), s32[]{:S(2)}) async-start(), calls=%async_computation.33 | async-start | bytes 1114112 | tf_op jit(solution)/shard_map/reduce_scatter | solution.py:194
  1062.9 165.1 %reduce-scatter.41.cloned.1.call-start = ((), (), s32[]{:S(2)}) async-start(), calls=%async_computation.34 | async-start | bytes 1114112 | tf_op jit(solution)/shard_map/reduce_scatter | solution.py:194
  1133.2 248.3 %all-reduce.9.cloned.1.call-start = ((), (), s32[]{:S(2)}) async-start(), calls=%async_computation.35 | async-start | bytes 17301504 | tf_op jit(solution)/shard_map/psum | solution.py:197
  (60 other events, 467.9 us)
Sparse Core Ops, SparseCore 0:
  10.2 40.6 all-gather.8
  59.8 9.1 reduce-scatter.14
  71.2 37.9 all-gather.10
  118.1 9.1 reduce-scatter.16
  129.3 37.9 all-gather.12
  176.2 9.1 reduce-scatter.18
  187.5 37.9 all-gather.14
  234.4 9.1 reduce-scatter.20
  245.7 37.9 all-gather.16
  292.6 9.1 reduce-scatter.22
  304.0 37.9 all-gather.18
  350.8 9.1 reduce-scatter.24
  362.2 37.9 all-gather.20
  409.0 9.1 reduce-scatter.26
  705.4 57.4 reduce-scatter.28
  777.7 56.4 reduce-scatter.30
  849.0 56.3 reduce-scatter.32
  920.2 56.4 reduce-scatter.34
  991.9 56.2 reduce-scatter.36
  1063.0 56.4 reduce-scatter.38
  1133.3 56.4 reduce-scatter.40
  1198.5 183.0 all-reduce.8
where the time goes:
time: 1410 us; the launch traced here: 1400 us
  waiting for transfers between devices  819 us (58%)
  matrix products  292 us (21%)
  local copies, waits for them, and re-layouts  160 us (11%)
  blocking collectives  76.8 us (5%)
  other arithmetic  31.6 us (2%)
  between operations  16.6 us (1%)
    reduce_scatter x7, waiting for transfers between devices, per_device(): lax.psum_scatter(partial_value, 'row', scatter_dimension=0, tiled=True)  329 us
    all_gather x7, waiting for transfers between devices, per_device(): lax.all_gather(field, 'row', axis=0, tiled=True)  276 us
    psum x1, waiting for transfers between devices, per_device(): lax.psum((grad_w_input, grad_bias_input, grad_gain_attn, grad_shift_attn,...  152 us
    reduce_scatter x7, waiting for transfers between devices, per_device(): lax.psum_scatter(forward_partial_value, 'col', scatter_dimension=0, tiled...  61.6 us
    dot_general x3, matrix products, node_tail(): projected = jnp.einsum('ntd,de->nte', normed, w_heads, precision=exact)  57.1 us
    psum x1, blocking collectives, per_device(): lax.psum((grad_w_input, grad_bias_input, grad_gain_attn, grad_shift_attn,...  41.8 us
    dot_general x3, matrix products, node_tail(): jnp.einsum('nhqk,nkhe->nqhe', attention, value_rows, precision=exact)  39.7 us
    dot_general x3, matrix products, node_tail(): jnp.einsum('nqhe,nkhe->nhqk', queries, key_rows, precision=exact)  37 us
  transfers between devices with their start and end apart: 22, of which 21 were waited for; matrix products, arithmetic and copies ran while one was open for 5% of the time, Pallas kernels for 0%

commit v1 on v0

--- a/solution.py
+++ b/solution.py
@@ -194,7 +194,7 @@
         carried = grad_hops[:, hop_index] + lax.psum_scatter(
             partial_value, "row", scatter_dimension=0, tiled=True
         )
-    summed = lax.psum(
+    one_axis = lax.psum(
         (
             grad_w_input,
             grad_bias_input,
@@ -211,8 +211,9 @@
             grad_bias_reduce,
             grad_readout,
         ),
-        ("row", "col"),
-    )
+        "col",
+    )
+    summed = lax.psum(one_axis, "row")
     return (
         layer_out,
         carried,

time: 1410 us -> 1600 us (1.13)
  waiting for transfers between devices: 819 us -> 981 us
  blocking collectives: 76.8 us -> 102 us
    psum x0 -> x1, waiting for transfers between devices: none -> 162 us  [per_device(): summed = lax.psum(one_axis, 'row')]
    psum x0 -> x1, blocking collectives: none -> 60.1 us  [per_device(): summed = lax.psum(one_axis, 'row')]
    psum x1, waiting for transfers between devices: 152 us -> 196 us  [per_device(): lax.psum((grad_w_input, grad_bias_input, grad_gain_attn, grad_shift_attn,...]
    reduce_scatter x7, waiting for transfers between devices: 329 us -> 286 us  [per_device(): lax.psum_scatter(partial_value, 'row', scatter_dimension=0, tiled=True)]
    psum x1, blocking collectives: 41.8 us -> 7.07 us  [per_device(): lax.psum((grad_w_input, grad_bias_input, grad_gain_attn, grad_shift_attn,...]
  transfers between devices with their start and end apart: 22 -> 23, of which waited for: 21 -> 22; matrix products, arithmetic and copies ran while one was open for 5% -> 5% of each run, Pallas kernels for 0% -> 0%
where the time goes in v1:
time: 1600 us; the launch traced here: 1580 us
  waiting for transfers between devices  981 us (61%)
  matrix products  292 us (18%)
  local copies, waits for them, and re-layouts  161 us (10%)
  blocking collectives  102 us (6%)
  other arithmetic  31.6 us (2%)
  between operations  16.4 us (1%)
    reduce_scatter x7, waiting for transfers between devices, per_device(): lax.psum_scatter(partial_value, 'row', scatter_dimension=0, tiled=True)  286 us
    all_gather x7, waiting for transfers between devices, per_device(): lax.all_gather(field, 'row', axis=0, tiled=True)  275 us
    psum x1, waiting for transfers between devices, per_device(): lax.psum((grad_w_input, grad_bias_input, grad_gain_attn, grad_shift_attn,...  196 us
    psum x1, waiting for transfers between devices, per_device(): summed = lax.psum(one_axis, 'row')  162 us
    reduce_scatter x7, waiting for transfers between devices, per_device(): lax.psum_scatter(forward_partial_value, 'col', scatter_dimension=0, tiled...  61.6 us
    psum x1, blocking collectives, per_device(): summed = lax.psum(one_axis, 'row')  60.1 us
    dot_general x3, matrix products, node_tail(): projected = jnp.einsum('ntd,de->nte', normed, w_heads, precision=exact)  57.1 us
    dot_general x3, matrix products, node_tail(): jnp.einsum('nhqk,nkhe->nqhe', attention, value_rows, precision=exact)  39.7 us
  transfers between devices with their start and end apart: 23, of which 22 were waited for; matrix products, arithmetic and copies ran while one was open for 5% of the time, Pallas kernels for 0%

profile of v1, /device:TPU:0, one launch (start us, length us, event | category | flops | bytes accessed | tf_op | source)
XLA Modules:
  0.0 1584.9 jit_solution(1265483429094064749)
XLA Ops:
  9.5 41.4 %all-gather.9.cloned.1.call-done = f32[2048,128]{1,0:T(8,128)} async-done(((f32[128,128]{1,0:T(8,128)}), f32[2048,128]{1,0:T(8,128)}) %all-gather.9.cloned.1.call-update) | async-done | bytes 1048592 | tf_op jit(solution)/shard_map/all_gather | solution.py:101
  59.8 9.3 reduce-scatter.15.cloned.1.call-done
  69.1 40.1 %all-gather.11.cloned.1.call-done = f32[2048,128]{1,0:T(8,128)} async-done(((f32[128,128]{1,0:T(8,128)}), f32[2048,128]{1,0:T(8,128)}) %all-gather.11.cloned.1.call-update) | async-done | bytes 1048592 | tf_op jit(solution)/shard_map/all_gather | solution.py:101
  127.4 39.9 %all-gather.13.cloned.1.call-done = f32[2048,128]{1,0:T(8,128)} async-done(((f32[128,128]{1,0:T(8,128)}), f32[2048,128]{1,0:T(8,128)}) %all-gather.13.cloned.1.call-update) | async-done | bytes 1048592 | tf_op jit(solution)/shard_map/all_gather | solution.py:101
  185.4 40.1 %all-gather.15.cloned.1.call-done = f32[2048,128]{1,0:T(8,128)} async-done(((f32[128,128]{1,0:T(8,128)}), f32[2048,128]{1,0:T(8,128)}) %all-gather.15.cloned.1.call-update) | async-done | bytes 1048592 | tf_op jit(solution)/shard_map/all_gather | solution.py:101
  234.3 9.3 reduce-scatter.21.cloned.1.call-done
  243.7 40.1 %all-gather.17.cloned.1.call-done = f32[2048,128]{1,0:T(8,128)} async-done(((f32[128,128]{1,0:T(8,128)}), f32[2048,128]{1,0:T(8,128)}) %all-gather.17.cloned.1.call-update) | async-done | bytes 1048592 | tf_op jit(solution)/shard_map/all_gather | solution.py:101
  301.9 40.1 %all-gather.19.cloned.1.call-done = f32[2048,128]{1,0:T(8,128)} async-done(((f32[128,128]{1,0:T(8,128)}), f32[2048,128]{1,0:T(8,128)}) %all-gather.19.cloned.1.call-update) | async-done | bytes 1048592 | tf_op jit(solution)/shard_map/all_gather | solution.py:101
  366.4 33.8 %all-gather.21.cloned.1.call-done = f32[2048,128]{1,0:T(8,128)} async-done(((f32[128,128]{1,0:T(8,128)}), f32[2048,128]{1,0:T(8,128)}) %all-gather.21.cloned.1.call-update) | async-done | bytes 1048592 | tf_op jit(solution)/shard_map/all_gather | solution.py:101
  424.0 10.8 fusion.10
  434.9 14.4 fusion.197
  474.9 9.8 multiply_reduce_fusion.1
  488.9 10.2 convolution_bitcast_fusion.3
  519.3 9.3 fusion.2
  549.5 14.6 fusion.199
  587.1 16.1 %multiply_reduce_fusion = (f32[128,8,8]{2,1,0:T(8,128)}, f32[128,8,8,8]{2,3,1,0:T(8,128)}) fusion(f32[128,8,8]{2,1,0:T(8,128)} %multiply_divide_fusion, f32[128,8,8]{2,1,0:T(8,128)} %copy-done.20, f32[128,8,8,8]{2,3,1,0:T(8,128)} %copy-done.10, f32[128,8,64,8]{2,3,1,0:T(8,128)} %copy.74, f32[128,8,8,64]{3,1,2,0:T(8,128)} %copy.69), kind=kOutput, calls=%fused_computation.25 | convolution fusion | flops 50651136 | bytes 4816896 | tf_op jit(solution)/shard_map/transpose(jvp(nhqk,nkhe->nqhe))/dot_general | solution.py:45
  605.0 12.5 convolution_bitcast_fusion
  617.5 14.7 convolution_bitcast_fusion.1
  632.2 13.5 convolution_bitcast_fusion.2
  660.1 24.2 %fusion.194 = (f32[512]{0:T(512)}, f32[128,8]{0,1:T(8,128)S(1)}, f32[128,8,512]{2,0,1:T(8,128)S(1)}) fusion(f32[512]{0:T(512)S(1)} %copy-done.56, f32[128,8]{0,1:T(8,128)S(1)} %broadcast_multiply_fusion.1, f32[128,8,512]{2,0,1:T(8,128)} %copy-done.3, f32[512]{0:T(512)S(1)} %copy-done.42, f32[512,1536]{1,0:T(8,128)S(1)} %copy-done, ...), kind=kOutput, calls=%fused_computation.282 | convolution fusion | flops 9669965824 | bytes 13645824 | tf_op jit(solution)/shard_map/transpose(jvp(ntd,de->nte))/dot_general | solution.py:37
  705.4 57.5 %reduce-scatter.29.cloned.1.call-done = f32[128,128]{1,0:T(8,128)} async-done(((f32[2048,128]{1,0:T(8,128)}), f32[128,128]{1,0:T(8,128)}) %reduce-scatter.29.cloned.1.call-update) | async-done | bytes 65552 | tf_op jit(solution)/shard_map/reduce_scatter | solution.py:194
  777.7 56.6 %reduce-scatter.31.cloned.1.call-done = f32[128,128]{1,0:T(8,128)} async-done(((f32[2048,128]{1,0:T(8,128)}), f32[128,128]{1,0:T(8,128)}) %reduce-scatter.31.cloned.1.call-update) | async-done | bytes 65552 | tf_op jit(solution)/shard_map/reduce_scatter | solution.py:194
  849.0 56.6 %reduce-scatter.33.cloned.1.call-done = f32[128,128]{1,0:T(8,128)} async-done(((f32[2048,128]{1,0:T(8,128)}), f32[128,128]{1,0:T(8,128)}) %reduce-scatter.33.cloned.1.call-update) | async-done | bytes 65552 | tf_op jit(solution)/shard_map/reduce_scatter | solution.py:194
  920.3 56.5 %reduce-scatter.35.cloned.1.call-done = f32[128,128]{1,0:T(8,128)} async-done(((f32[2048,128]{1,0:T(8,128)}), f32[128,128]{1,0:T(8,128)}) %reduce-scatter.35.cloned.1.call-update) | async-done | bytes 65552 | tf_op jit(solution)/shard_map/reduce_scatter | solution.py:194
  991.9 11.1 fusion.24
  1003.0 45.4 %reduce-scatter.37.cloned.1.call-done = f32[128,128]{1,0:T(8,128)} async-done(((f32[2048,128]{1,0:T(8,128)}), f32[128,128]{1,0:T(8,128)}) %reduce-scatter.37.cloned.1.call-update) | async-done | bytes 65552 | tf_op jit(solution)/shard_map/reduce_scatter | solution.py:194
  1074.2 10.3 convolution_bitcast_fusion.4
  1084.5 22.1 %fusion.8 = f32[512,1536]{1,0:T(8,128)} fusion(f32[128,8,512]{0,2,1:T(8,128)S(1)} %bitcast.343, f32[128,8,512]{0,2,1:T(8,128)S(1)} %bitcast.341, f32[128,8,512]{0,2,1:T(8,128)S(1)} %bitcast.339, f32[512]{0:T(512)S(1)} %copy-done.70, f32[512]{0:T(512)S(1)} %copy-done.57, f32[128,8]{0,1:T(8,128)S(1)} %copy-done.46, f32[128,8,512]{2,0,1:T(8,128)S(1)} %copy-done.5, ...), kind=kOutput, calls=%fused_computation.42 | convolution fusion | flops 9669443584 | bytes 11548672 | tf_op jit(solution)/shard_map/transpose(jvp(ntd,de->nte))/dot_general | solution.py:37
  1106.7 13.0 reduce-scatter.39.cloned.1.call-done
  1132.8 195.7 %all-reduce.14.cloned.1.call-done = (f32[128,512]{1,0:T(8,128)}, f32[512,1536]{1,0:T(8,128)}, f32[512,512]{1,0:T(8,128)}, f32[512,1024]{1,0:T(8,128)}, f32[1024,512]{1,0:T(8,128)}) async-done(((f32[128,512]{1,0:T(8,128)}, f32[512,1536]{1,0:T(8,128)}, f32[512,512]{1,0:T(8,128)}, f32[512,1024]{1,0:T(8,128)}, f32[1024,512]{1,0:T(8,128)}), (f32[128,512]{1,0:T(8,128)}, f32[512,1536]{1,0:T(8,128)}, ...) | async-done | bytes 8650768 | tf_op jit(solution)/shard_map/psum | solution.py:197
  1338.9 60.1 %all-reduce.5 = (f32[512]{0:T(512)}, f32[512]{0:T(512)}, f32[512]{0:T(512)}, f32[512]{0:T(512)}, f32[512]{0:T(512)}, /*index=5*/f32[512]{0:T(512)}, f32[1024]{0:T(1024)}, f32[512]{0:T(512)}, f32[512]{0:T(512)}) all-reduce(f32[512]{0:T(512)S(1)} %get-tuple-element.40, ...), channel_id=1, replica_groups=mesh['row'=16,'col'=2] {'row'}, use_global_device_ids=true, to_apply=%region_32.0 | all-reduce | flops 5120 | bytes 40960 | tf_op jit(solution)/shard_map/psum | solution.py:216
  1407.1 161.5 %all-reduce.12.cloned.1.call-done = (f32[128,512]{1,0:T(8,128)}, f32[512,1536]{1,0:T(8,128)}, f32[512,512]{1,0:T(8,128)}, f32[512,1024]{1,0:T(8,128)}, f32[1024,512]{1,0:T(8,128)}) async-done(((f32[128,512]{1,0:T(8,128)}, f32[512,1536]{1,0:T(8,128)}, f32[512,512]{1,0:T(8,128)}, f32[512,1024]{1,0:T(8,128)}, f32[1024,512]{1,0:T(8,128)}), (f32[128,512]{1,0:T(8,128)}, f32[512,1536]{1,0:T(8,128)}, ...) | async-done | bytes 8650768 | tf_op jit(solution)/shard_map/psum | solution.py:216
  (351 shorter events, 378.2 us)
Async XLA Ops:
  7.2 416.8 %copy-start = (f32[512,1536]{1,0:T(8,128)S(1)}, f32[512,1536]{1,0:T(8,128)}, u32[]{:S(2)}) copy-start(f32[512,1536]{1,0:T(8,128)} %param.29) | copy-start | bytes 9437188
  7.2 162.6 %copy-start.6 = (f32[1,1,4,128,128]{4,3,2,1,0:T(8,128)S(1)}, f32[1,1,4,128,128]{4,3,2,1,0:T(8,128)}, u32[]{:S(2)}) copy-start(f32[1,1,4,128,128]{4,3,2,1,0:T(8,128)} %param.21) | copy-start | bytes 786436
  7.2 108.6 %copy-start.52 = (s32[1,1,4]{2,1,0:T(1,128)S(1)}, s32[1,1,4]{2,1,0:T(1,128)}, u32[]{:S(2)}) copy-start(s32[1,1,4]{2,1,0:T(1,128)} %param.22) | copy-start | bytes 52
  7.2 43.7 %all-gather.9.cloned.1.call-start = ((), (), s32[]{:S(2)}) async-start(), calls=%async_computation.14 | async-start | bytes 1114112 | tf_op jit(solution)/shard_map/all_gather | solution.py:101
  8.0 61.1 %reduce-scatter.15.cloned.1.call-start = ((), (), s32[]{:S(2)}) async-start(), calls=%async_computation.15 | async-start | bytes 196608 | tf_op jit(solution)/shard_map/reduce_scatter | solution.py:110
  59.7 49.5 %all-gather.11.cloned.1.call-start = ((), (), s32[]{:S(2)}) async-start(), calls=%async_computation.16 | async-start | bytes 1114112 | tf_op jit(solution)/shard_map/all_gather | solution.py:101
  69.1 58.3 %reduce-scatter.17.cloned.1.call-start = ((), (), s32[]{:S(2)}) async-start(), calls=%async_computation.17 | async-start | bytes 196608 | tf_op jit(solution)/shard_map/reduce_scatter | solution.py:110
  118.0 49.3 %all-gather.13.cloned.1.call-start = ((), (), s32[]{:S(2)}) async-start(), calls=%async_computation.18 | async-start | bytes 1114112 | tf_op jit(solution)/shard_map/all_gather | solution.py:101
  127.3 58.0 %reduce-scatter.19.cloned.1.call-start = ((), (), s32[]{:S(2)}) async-start(), calls=%async_computation.19 | async-start | bytes 196608 | tf_op jit(solution)/shard_map/reduce_scatter | solution.py:110
  176.0 184.7 %copy-start.40 = (f32[128,128]{1,0:T(8,128)S(1)}, f32[128,128]{1,0:T(8,128)}, u32[]{:S(2)}) copy-start(f32[128,128]{1,0:T(8,128)} %param.20) | copy-start | bytes 196612
  176.0 185.3 %copy-start.41 = (f32[128,128]{1,0:T(8,128)S(1)}, f32[128,128]{1,0:T(8,128)}, u32[]{:S(2)}) copy-start(f32[128,128]{1,0:T(8,128)} %reduce-scatter.15.cloned.1.call-done) | copy-start | bytes 196612
  176.1 49.5 %all-gather.15.cloned.1.call-start = ((), (), s32[]{:S(2)}) async-start(), calls=%async_computation.20 | async-start | bytes 1114112 | tf_op jit(solution)/shard_map/all_gather | solution.py:101
  185.4 58.2 %reduce-scatter.21.cloned.1.call-start = ((), (), s32[]{:S(2)}) async-start(), calls=%async_computation.21 | async-start | bytes 196608 | tf_op jit(solution)/shard_map/reduce_scatter | solution.py:110
  234.3 49.5 %all-gather.17.cloned.1.call-start = ((), (), s32[]{:S(2)}) async-start(), calls=%async_computation.22 | async-start | bytes 1114112 | tf_op jit(solution)/shard_map/all_gather | solution.py:101
  243.6 58.2 %reduce-scatter.23.cloned.1.call-start = ((), (), s32[]{:S(2)}) async-start(), calls=%async_computation.23 | async-start | bytes 196608 | tf_op jit(solution)/shard_map/reduce_scatter | solution.py:110
  286.2 133.5 %copy-start.42 = (f32[512]{0:T(512)S(1)}, f32[512]{0:T(512)}, u32[]{:S(2)}) copy-start(f32[512]{0:T(512)} %param.26) | copy-start | bytes 6148
  292.5 49.5 %all-gather.19.cloned.1.call-start = ((), (), s32[]{:S(2)}) async-start(), calls=%async_computation.24 | async-start | bytes 1114112 | tf_op jit(solution)/shard_map/all_gather | solution.py:101
  301.8 58.2 %reduce-scatter.25.cloned.1.call-start = ((), (), s32[]{:S(2)}) async-start(), calls=%async_computation.25 | async-start | bytes 196608 | tf_op jit(solution)/shard_map/reduce_scatter | solution.py:110
  350.7 49.5 %all-gather.21.cloned.1.call-start = ((), (), s32[]{:S(2)}) async-start(), calls=%async_computation.26 | async-start | bytes 1114112 | tf_op jit(solution)/shard_map/all_gather | solution.py:101
  360.0 58.2 %reduce-scatter.27.cloned.1.call-start = ((), (), s32[]{:S(2)}) async-start(), calls=%async_computation.27 | async-start | bytes 196608 | tf_op jit(solution)/shard_map/reduce_scatter | solution.py:110
  362.0 62.1 %copy-start.69 = (f32[512]{0:T(512)S(1)}, f32[512]{0:T(512)}, u32[]{:S(2)}) copy-start(f32[512]{0:T(512)} %param.28) | copy-start | bytes 6148
  408.9 354.1 %reduce-scatter.29.cloned.1.call-start = ((), (), s32[]{:S(2)}) async-start(), calls=%async_computation.28 | async-start | bytes 1114112 | tf_op jit(solution)/shard_map/reduce_scatter | solution.py:194
  424.0 262.1 %copy-start.45 = (f32[128,8]{0,1:T(8,128)}, f32[128,8]{0,1:T(8,128)S(1)}, u32[]{:S(2)}) copy-start(f32[128,8]{0,1:T(8,128)S(1)} %fusion.126) | copy-start | bytes 12292
  511.2 62.4 %copy-start.47 = (f32[128,8]{0,1:T(8,128)}, f32[128,8]{0,1:T(8,128)S(1)}, u32[]{:S(2)}) copy-start(f32[128,8]{0,1:T(8,128)S(1)} %fusion.127) | copy-start | bytes 12292
  705.4 128.9 %reduce-scatter.31.cloned.1.call-start = ((), (), s32[]{:S(2)}) async-start(), calls=%async_computation.29 | async-start | bytes 1114112 | tf_op jit(solution)/shard_map/reduce_scatter | solution.py:194
  777.7 127.9 %reduce-scatter.33.cloned.1.call-start = ((), (), s32[]{:S(2)}) async-start(), calls=%async_computation.30 | async-start | bytes 1114112 | tf_op jit(solution)/shard_map/reduce_scatter | solution.py:194
  849.0 127.8 %reduce-scatter.35.cloned.1.call-start = ((), (), s32[]{:S(2)}) async-start(), calls=%async_computation.31 | async-start | bytes 1114112 | tf_op jit(solution)/shard_map/reduce_scatter | solution.py:194
  920.3 128.2 %reduce-scatter.37.cloned.1.call-start = ((), (), s32[]{:S(2)}) async-start(), calls=%async_computation.32 | async-start | bytes 1114112 | tf_op jit(solution)/shard_map/reduce_scatter | solution.py:194
  991.9 127.8 %reduce-scatter.39.cloned.1.call-start = ((), (), s32[]{:S(2)}) async-start(), calls=%async_computation.33 | async-start | bytes 1114112 | tf_op jit(solution)/shard_map/reduce_scatter | solution.py:194
  1063.1 265.4 %all-reduce.14.cloned.1.call-start = ((), (), s32[]{:S(2)}) async-start(), calls=%async_computation.36 | async-start | bytes 17301504 | tf_op jit(solution)/shard_map/psum | solution.py:197
  1106.6 298.9 %reduce-scatter.41.cloned.1.call-start = ((), (), s32[]{:S(2)}) async-start(), calls=%async_computation.34 | async-start | bytes 1114112 | tf_op jit(solution)/shard_map/reduce_scatter | solution.py:194
  1132.7 435.9 %all-reduce.12.cloned.1.call-start = ((), (), s32[]{:S(2)}) async-start(), calls=%async_computation.35 | async-start | bytes 17301504 | tf_op jit(solution)/shard_map/psum | solution.py:216
  (62 other events, 553.2 us)
Sparse Core Ops, SparseCore 0:
  10.2 40.6 all-gather.8
  59.8 9.1 reduce-scatter.14
  71.2 37.9 all-gather.10
  118.1 9.1 reduce-scatter.16
  129.3 37.9 all-gather.12
  176.2 9.1 reduce-scatter.18
  187.5 37.9 all-gather.14
  234.4 9.1 reduce-scatter.20
  245.7 37.9 all-gather.16
  292.6 9.1 reduce-scatter.22
  304.0 37.9 all-gather.18
  350.8 9.1 reduce-scatter.24
  362.2 37.9 all-gather.20
  409.0 9.1 reduce-scatter.26
  705.5 57.4 reduce-scatter.28
  777.8 56.4 reduce-scatter.30
  849.1 56.4 reduce-scatter.32
  920.4 56.3 reduce-scatter.34
  992.0 56.4 reduce-scatter.36
  1063.3 56.3 reduce-scatter.38
  1123.7 204.7 all-reduce.13
  1332.7 57.4 reduce-scatter.40
  1395.0 173.5 all-reduce.11
